TPU v7x, 256 devices: a whole 4x4x8 slice. The times are simulated.
256 devices in a mesh: rep: 16 (over x, z_hi), tp: 16 (over y, z_lo, core).
Axes of the slice: x: 4, y: 4, z: 8 (z_hi: 4, z_lo: 2; z = z_hi * 2 + z_lo), core: 2. Of those that a mesh axis runs over, the one named last changes fastest.
Arguments:
- hidden: bfloat16 [8192, 8192], P(('rep', 'tp')), may hold values from -6 to 6
- norm_gain: bfloat16 [8192], replicated, may hold values from 0.099609375 to 1.8984375
- q_weight: bfloat16 [8192, 8192], P('rep', 'tp')
- kv_weight: bfloat16 [8192, 2048], P('rep'), may hold values from -0.0625 to 0.0625
- out_weight: bfloat16 [8192, 8192], P('tp', 'rep'), may hold values from -0.0625 to 0.0625
- held_slice: int32 [16], replicated, may hold values from 0 to 15, each once
Outputs:
- attended: bfloat16 [8192, 8192], P(('rep', 'tp'))
Inputs may be any that keep to these rules, and one draw needn't show every extreme that they name: `held_slice`: each slice number appears once.
All inputs are finite; a program needn't handle non-finite values.
Results may differ from a plain program's by a relative error of at most 0.019.
The roundings to bfloat16 on the way count: a program that leaves them out, or rounds other values in their place, can miss the bound.
Values may be sent and summed in bfloat16 or wider, within the bound.
A program may use at most 128 MiB of HBM per device.

v0:
```python
import jax
import jax.numpy as jnp
from jax import lax
from jax.sharding import PartitionSpec as P

HD = 128
HQ = 64
KVH = 8
rope_theta = 500000.0


def side_by_side(arrays, axis, dim, along):
    both = jnp.concatenate(arrays, axis=along)
    result, at, done = (lax.all_gather(both, axis, axis=dim, tiled=True), 0, [])
    for a in arrays:
        done.append(lax.slice_in_dim(result, at, at + a.shape[along], axis=along))
        at += a.shape[along]
    return tuple(done)


def rotate(states, positions):
    half = states.shape[-1] // 2
    freqs = rope_theta ** (-(jnp.arange(half, dtype=jnp.float32) * 2.0) / states.shape[-1])
    angles = positions[:, None] * freqs[None, :]
    cosine = jnp.cos(angles)[:, None, :]
    sine = jnp.sin(angles)[:, None, :]
    first = states[..., :half]
    second = states[..., half:]
    return jnp.concatenate(
        [first * cosine - second * sine, second * cosine + first * sine], axis=-1
    )


def attend(queries, keys, values):
    row_count = queries.shape[0]
    kv_local = keys.shape[1]
    per_group = queries.shape[1] // kv_local
    head_size = queries.shape[-1]
    positions = jnp.arange(row_count, dtype=jnp.int32)
    scale = 1.0 / head_size**0.5
    grouped = queries.reshape(row_count, kv_local, per_group, head_size)
    scores = jnp.einsum("sgqd,tgd->gqst", grouped, keys, preferred_element_type=jnp.float32) * scale
    allowed = positions[:, None] >= positions[None, :]
    scores = jnp.where(allowed[None, None, :, :], scores, -1e30)
    peak = jnp.max(scores, axis=-1, keepdims=True)
    weights = jnp.exp(scores - peak)
    probs = (weights / jnp.sum(weights, axis=-1, keepdims=True)).astype(jnp.bfloat16)
    context = jnp.einsum("gqst,tgd->sgqd", probs, values, preferred_element_type=jnp.float32)
    return context.astype(jnp.bfloat16).reshape(row_count, -1)


def per_device(hidden, norm_gain, q_weight, kv_weight, out_weight, held_slice):
    states = hidden.astype(jnp.float32)
    meansq = jnp.mean(states * states, axis=-1, keepdims=True)
    normed = (states * lax.rsqrt(meansq + 1e-05) * norm_gain.astype(jnp.float32)).astype(
        jnp.bfloat16
    )
    gathered = lax.all_gather(normed, "tp", axis=0, tiled=True)
    row_count = gathered.shape[0]
    width = gathered.shape[1]
    part_count = lax.axis_size("rep")
    slice_rows = width // part_count
    query_cols = q_weight.shape[1]
    heads_here = query_cols // HD
    group_size = HQ // KVH
    kv_local = max(1, heads_here // group_size)
    first_shared = lax.axis_index("tp") * heads_here // group_size
    key_cols = lax.dynamic_slice_in_dim(kv_weight, first_shared * HD, kv_local * HD, 1)
    value_cols = lax.dynamic_slice_in_dim(kv_weight, KVH * HD + first_shared * HD, kv_local * HD, 1)
    pair_cols = jnp.concatenate([key_cols, value_cols], axis=1)
    inverse = (
        jnp.zeros((part_count,), jnp.int32)
        .at[held_slice]
        .set(jnp.arange(part_count, dtype=jnp.int32))
    )
    blocks = gathered.reshape(row_count, part_count, slice_rows)
    pieces = side_by_side((q_weight, pair_cols), "rep", 0, 1)
    taken = pieces[0].shape[0] // slice_rows
    chosen = jnp.take(blocks, held_slice, axis=1).reshape(row_count, taken * slice_rows)
    queries = jnp.dot(chosen, pieces[0], preferred_element_type=jnp.float32)
    pairs = jnp.dot(chosen, pieces[1], preferred_element_type=jnp.float32)
    out_all = lax.all_gather(out_weight, "rep", axis=1, tiled=True)
    out_ordered = jnp.take(
        out_all.reshape(query_cols, part_count, slice_rows), inverse, axis=1
    ).reshape(query_cols, width)
    where_at = jnp.arange(row_count, dtype=jnp.float32)
    queries = rotate(queries.reshape(row_count, heads_here, HD), where_at).astype(jnp.bfloat16)
    keys = rotate(pairs[:, : kv_local * HD].reshape(row_count, kv_local, HD), where_at).astype(
        jnp.bfloat16
    )
    values = pairs[:, kv_local * HD :].reshape(row_count, kv_local, HD).astype(jnp.bfloat16)
    context = attend(queries, keys, values)
    partial_value = jnp.dot(context, out_ordered, preferred_element_type=jnp.float32)
    summed = lax.psum_scatter(
        partial_value.astype(jnp.bfloat16), "tp", scatter_dimension=0, tiled=True
    )
    return summed


def solution(mesh):
    return jax.shard_map(
        per_device,
        mesh=mesh,
        in_specs=(P(("rep", "tp"), None), P(), P("rep", "tp"), P("rep", None), P("tp", "rep"), P()),
        out_specs=P(("rep", "tp"), None),
        check_vma=False,
    )
```

profile of v0, /device:TPU:2, one launch (start us, length us, event | category | flops | bytes accessed | tf_op | source)
XLA Modules:
  0.0 501.7 jit_solution(620382676256943983)
XLA Ops:
  6.5 0.0 all-gather.4.cloned.1.call-start
  6.5 1.2 fusion.10
  7.8 0.7 convert_element_type.34
  8.5 2.0 fusion.12
  10.5 0.0 all-gather.4.cloned.1.call-update
  10.6 0.0 all-gather.8.cloned.1.call-start
  10.6 2.1 copy.34
  12.7 0.0 all-gather.8.cloned.1.call-update
  12.7 0.0 all-gather.6.cloned.1.call-start
  12.8 1.0 constant_dynamic-slice_fusion.1
  13.8 2.0 pad_maximum_fusion
  15.8 0.0 all-gather.6.cloned.1.call-update
  15.8 0.0 reduce-scatter.2.cloned.1.call-start
  15.9 0.7 compare_select_fusion.1
  16.5 0.6 scatter_custom_fusion
  17.2 0.1 iota_compare_fusion
  17.3 0.7 compare_and_fusion
  18.0 0.5 fusion.22
  18.5 49.8 %all-gather.4.cloned.1.call-done = bf16[512,8192]{1,0:T(8,128)(2,1)} async-done(((bf16[32,8192]{1,0:T(8,128)(2,1)}), bf16[512,8192]{1,0:T(8,128)(2,1)}) %all-gather.4.cloned.1.call-update) | async-done | bytes 8388624 | tf_op jit(solution)/shard_map/all_gather | solution.py:58
  68.3 12.0 %copy.26 = bf16[512,8192]{0,1:T(8,128)(2,1)} copy(bf16[512,8192]{1,0:T(8,128)(2,1)} %all-gather.4.cloned.1.call-done) | data formatting | bytes 16777216 | tf_op jit(solution)/shard_map/all_gather | solution.py:58
  80.3 12.2 %copy.27 = bf16[512,16,512]{2,0,1:T(8,128)(2,1)} copy(bf16[512,16,512]{0,2,1:T(8,128)(2,1)} %bitcast.58) | data formatting | bytes 16777216 | tf_op jit(solution)/shard_map/reshape | solution.py:76
  92.5 8.5 %gather_fusion = bf16[16,512,512]{2,1,0:T(8,128)(2,1)} fusion(bf16[512,16,512]{2,0,1:T(8,128)(2,1)} %copy.27, s32[1024]{0:T(1024)S(1)} %pad_clamp_fusion.1), kind=kCustom, calls=%fused_computation.clone | custom fusion | bytes 16777280 | tf_op jit(solution)/shard_map/jit(_take)/gather | solution.py:79
  100.9 7.6 %select_bitcast_fusion.1 = bf16[512,16,512]{2,0,1:T(8,128)(2,1)} fusion(bf16[16,512,512]{2,1,0:T(8,128)(2,1)} %gather_fusion, pred[16]{0:T(512)(128)(4,1)S(1)} %get-tuple-element.17), kind=kLoop, calls=%fused_computation.6 | loop fusion | flops 4194304 | bytes 16777232 | tf_op jit(solution)/shard_map/jit(_take)/select_n | solution.py:79
  108.6 12.3 %copy.28 = bf16[512,16,512]{0,2,1:T(8,128)(2,1)} copy(bf16[512,16,512]{2,0,1:T(8,128)(2,1)} %select_bitcast_fusion.1) | data formatting | bytes 16777216 | tf_op jit(solution)/shard_map/jit(_take)/select_n | solution.py:79
  120.9 59.8 %all-gather.8.cloned.1.call-done = bf16[512,8192]{0,1:T(8,128)(2,1)} async-done(((bf16[512,512]{0,1:T(8,128)(2,1)}), bf16[512,8192]{0,1:T(8,128)(2,1)}) %all-gather.8.cloned.1.call-update) | async-done | bytes 8388624 | tf_op jit(solution)/shard_map/all_gather | solution.py:82
  180.7 12.3 %copy.35 = bf16[512,16,512]{2,0,1:T(8,128)(2,1)} copy(bf16[512,16,512]{0,2,1:T(8,128)(2,1)} %bitcast.59) | data formatting | bytes 16777216 | tf_op jit(solution)/shard_map/reshape | solution.py:84
  193.0 8.1 %gather_fusion.1 = bf16[16,512,512]{2,1,0:T(8,128)(2,1)} fusion(bf16[512,16,512]{2,0,1:T(8,128)(2,1)} %copy.35, s32[1024]{0:T(1024)S(1)} %pad_clamp_fusion), kind=kCustom, calls=%fused_computation.1.clone | custom fusion | bytes 16777280 | tf_op jit(solution)/shard_map/jit(_take)/gather | solution.py:83
  201.1 8.2 %select_bitcast_fusion = bf16[512,16,512]{2,0,1:T(8,128)(2,1)} fusion(bf16[16,512,512]{2,1,0:T(8,128)(2,1)} %gather_fusion.1, pred[16]{0:T(512)(128)(4,1)S(1)} %get-tuple-element.16), kind=kLoop, calls=%fused_computation.5 | loop fusion | flops 4194304 | bytes 16777232 | tf_op jit(solution)/shard_map/jit(_take)/select_n | solution.py:83
  209.3 12.3 %copy.36 = bf16[512,16,512]{0,2,1:T(8,128)(2,1)} copy(bf16[512,16,512]{2,0,1:T(8,128)(2,1)} %select_bitcast_fusion) | data formatting | bytes 16777216 | tf_op jit(solution)/shard_map/jit(_take)/select_n | solution.py:83
  221.6 116.4 %all-gather.6.cloned.1.call-done = bf16[8192,768]{1,0:T(8,128)(2,1)} async-done(((bf16[512,768]{1,0:T(8,128)(2,1)}), bf16[8192,768]{1,0:T(8,128)(2,1)}) %all-gather.6.cloned.1.call-update) | async-done | bytes 12582928 | tf_op jit(solution)/shard_map/all_gather | solution.py:14
  338.0 7.1 %slice_bitcast_fusion = bf16[512,8192]{0,1:T(8,128)(2,1)} fusion(bf16[8192,768]{1,0:T(8,128)(2,1)} %all-gather.6.cloned.1.call-done), kind=kLoop, calls=%fused_computation.4 | loop fusion | bytes 16777216 | tf_op jit(solution)/shard_map/dot_general | solution.py:80
  345.1 11.4 %copy.29 = bf16[512,8192]{1,0:T(8,128)(2,1)} copy(bf16[512,8192]{0,1:T(8,128)(2,1)} %slice_bitcast_fusion) | data formatting | bytes 16777216 | tf_op jit(solution)/shard_map/dot_general | solution.py:80
  356.6 0.0 copy-start
  356.6 7.1 %fusion = f32[512,256]{0,1:T(8,128)S(1)} fusion(bf16[512,8192]{0,1:T(8,128)(2,1)} %bitcast.61, bf16[8192,768]{1,0:T(8,128)(2,1)} %all-gather.6.cloned.1.call-done), kind=kOutput, calls=%fused_computation.7 | convolution fusion | flops 2147483648 | bytes 13107200 | tf_op jit(solution)/shard_map/dot_general | solution.py:81
  363.7 0.6 fusion.25
  364.2 0.0 copy-done
  364.3 7.3 %fusion.32 = f32[512,4,128]{0,2,1:T(8,128)S(1)} fusion(bf16[512,8192,1]{0,1,2:T(8,128)(2,1)} %bitcast.62, bf16[4,128,8192]{2,1,0:T(8,128)(2,1)S(1)} %bitcast.63), kind=kOutput, calls=%fused_computation.62 | convolution fusion | flops 4294967296 | bytes 17825792 | tf_op jit(solution)/shard_map/dot_general | solution.py:80
  371.5 0.2 subtract_convert_fusion
  371.7 0.9 fusion.3
  372.6 0.9 fusion.2
  373.6 1.5 fusion.7
  375.1 10.2 %convolution_convert_fusion = bf16[512,8192]{1,0:T(8,128)(2,1)} fusion(bf16[512,512]{0,1:T(8,128)(2,1)S(1)} %bitcast.64, bf16[512,8192]{0,1:T(8,128)(2,1)} %bitcast.60), kind=kOutput, calls=%fused_computation.3 | convolution fusion | flops 4299161600 | bytes 17301504 | tf_op jit(solution)/shard_map/dot_general | solution.py:93
  385.3 0.0 reduce-scatter.2.cloned.1.call-update
  385.3 109.8 %reduce-scatter.2.cloned.1.call-done = bf16[32,8192]{1,0:T(8,128)(2,1)} async-done(((bf16[512,8192]{1,0:T(8,128)(2,1)}), bf16[32,8192]{1,0:T(8,128)(2,1)}) %reduce-scatter.2.cloned.1.call-update) | async-done | bytes 524304 | tf_op jit(solution)/shard_map/reduce_scatter | solution.py:94
  (7 shorter events, 0.1 us)
Async XLA Ops:
  6.5 61.8 %all-gather.4.cloned.1.call-start = ((), (), s32[]{:S(2)}) async-start(), calls=%async_computation.1 | async-start | bytes 8912896 | tf_op jit(solution)/shard_map/all_gather | solution.py:58
  10.6 170.1 %all-gather.8.cloned.1.call-start = ((), (), s32[]{:S(2)}) async-start(), calls=%async_computation.3 | async-start | bytes 8912896 | tf_op jit(solution)/shard_map/all_gather | solution.py:82
  12.7 325.3 %all-gather.6.cloned.1.call-start = ((), (), s32[]{:S(2)}) async-start(), calls=%async_computation.2 | async-start | bytes 13369344 | tf_op jit(solution)/shard_map/all_gather | solution.py:14
  15.8 479.4 %reduce-scatter.2.cloned.1.call-start = ((), (), s32[]{:S(2)}) async-start(), calls=%async_computation.4 | async-start | bytes 8912896 | tf_op jit(solution)/shard_map/reduce_scatter | solution.py:94
  356.6 7.7 %copy-start = (bf16[512,8192]{1,0:T(8,128)(2,1)S(1)}, bf16[512,8192]{1,0:T(8,128)(2,1)}, u32[]{:S(2)}) copy-start(bf16[512,8192]{1,0:T(8,128)(2,1)} %copy.29) | copy-start | bytes 25165828
Sparse Core Ops, SparseCore 0:
  10.7 57.5 all-gather.3
  70.8 109.8 all-gather.7
  183.2 154.7 all-gather.5
  385.4 109.6 reduce-scatter.1
where the time goes:
time: 504 us; the launch traced here: 502 us
  waiting for transfers between devices  336 us (67%)
  local copies, waits for them, and re-layouts  99.9 us (20%)
  matrix products  27 us (5%)
  other arithmetic  25.4 us (5%)
  between operations  13.3 us (3%)
    all_gather x1, waiting for transfers between devices, side_by_side(): result, at, done = (lax.all_gather(both, axis, axis=dim, tiled=True), 0, [])  116 us
    reduce_scatter x1, waiting for transfers between devices, per_device(): lax.psum_scatter(partial_value.astype(jnp.bfloat16), 'tp', scatter_dimens...  110 us
    all_gather x1, waiting for transfers between devices, per_device(): out_all = lax.all_gather(out_weight, 'rep', axis=1, tiled=True)  59.8 us
    all_gather x1, waiting for transfers between devices, per_device(): gathered = lax.all_gather(normed, 'tp', axis=0, tiled=True)  49.8 us
    dot_general x2, local copies, waits for them, and re-layouts, per_device(): queries = jnp.dot(chosen, pieces[0], preferred_element_type=jnp.float32)  18.6 us
    select_n x1, local copies, waits for them, and re-layouts, per_device(): jnp.take(out_all.reshape(query_cols, part_count, slice_rows), inverse, ax...  12.3 us
    select_n x1, local copies, waits for them, and re-layouts, per_device(): jnp.take(blocks, held_slice, axis=1).reshape(row_count, taken * slice_rows)  12.3 us
    reshape x1, local copies, waits for them, and re-layouts, per_device(): out_all.reshape(query_cols, part_count, slice_rows)  12.3 us
  transfers between devices with their start and end apart: 4, of which 4 were waited for; matrix products, arithmetic and copies ran while one was open for 20% of the time, Pallas kernels for 0%

commit v1 on v0

--- a/solution.py
+++ b/solution.py
@@ -79,7 +79,9 @@
     chosen = jnp.take(blocks, held_slice, axis=1).reshape(row_count, taken * slice_rows)
     queries = jnp.dot(chosen, pieces[0], preferred_element_type=jnp.float32)
     pairs = jnp.dot(chosen, pieces[1], preferred_element_type=jnp.float32)
-    out_all = lax.all_gather(out_weight, "rep", axis=1, tiled=True)
+    out_all = jnp.concatenate(
+        lax.all_to_all(jnp.stack([out_weight] * lax.axis_size("rep")), "rep", 0, 0), axis=1
+    )
     out_ordered = jnp.take(
         out_all.reshape(query_cols, part_count, slice_rows), inverse, axis=1
     ).reshape(query_cols, width)

time: 504 us -> 545 us (1.081)
  waiting for transfers between devices: 336 us -> 378 us
  starting transfers between devices: 0.13 us -> 11.7 us
  local copies, waits for them, and re-layouts: 99.9 us -> 90.1 us
    all_gather x1, waiting for transfers between devices: 49.8 us -> 150 us  [per_device(): gathered = lax.all_gather(normed, 'tp', axis=0, tiled=True)]
    all_gather x1 -> x0, waiting for transfers between devices: 59.8 us -> none  [per_device(): out_all = lax.all_gather(out_weight, 'rep', axis=1, tiled=True)]
    all_gather x1, waiting for transfers between devices: 116 us -> 78.7 us  [side_by_side(): result, at, done = (lax.all_gather(both, axis, axis=dim, tiled=True), 0, [])]
    all_to_all x0 -> x1, waiting for transfers between devices: none -> 34.9 us  [per_device(): lax.all_to_all(jnp.stack([out_weight] * lax.axis_size('rep')), 'rep', 0, 0)]
    reshape x1 -> x0, local copies, waits for them, and re-layouts: 12.3 us -> none  [per_device(): out_all.reshape(query_cols, part_count, slice_rows)]
    all_to_all x0 -> x1, starting transfers between devices: none -> 11.6 us  [per_device(): lax.all_to_all(jnp.stack([out_weight] * lax.axis_size('rep')), 'rep', 0, 0)]
  transfers between devices with their start and end apart: 4 -> 4, of which waited for: 4 -> 4; matrix products, arithmetic and copies ran while one was open for 20% -> 16% of each run, Pallas kernels for 0% -> 0%
where the time goes in v1:
time: 545 us; the launch traced here: 543 us
  waiting for transfers between devices  378 us (69%)
  local copies, waits for them, and re-layouts  90.1 us (17%)
  matrix products  27 us (5%)
  other arithmetic  23.4 us (4%)
  between operations  13.3 us (2%)
  starting transfers between devices  11.7 us (2%)
    all_gather x1, waiting for transfers between devices, per_device(): gathered = lax.all_gather(normed, 'tp', axis=0, tiled=True)  150 us
    reduce_scatter x1, waiting for transfers between devices, per_device(): lax.psum_scatter(partial_value.astype(jnp.bfloat16), 'tp', scatter_dimens...  114 us
    all_gather x1, waiting for transfers between devices, side_by_side(): result, at, done = (lax.all_gather(both, axis, axis=dim, tiled=True), 0, [])  78.7 us
    all_to_all x1, waiting for transfers between devices, per_device(): lax.all_to_all(jnp.stack([out_weight] * lax.axis_size('rep')), 'rep', 0, 0)  34.9 us
    dot_general x2, local copies, waits for them, and re-layouts, per_device(): queries = jnp.dot(chosen, pieces[0], preferred_element_type=jnp.float32)  18.6 us
    reshape x1, local copies, waits for them, and re-layouts, per_device(): blocks = gathered.reshape(row_count, part_count, slice_rows)  12.3 us
    select_n x1, local copies, waits for them, and re-layouts, per_device(): jnp.take(blocks, held_slice, axis=1).reshape(row_count, taken * slice_rows)  12.3 us
    all_gather x1, local copies, waits for them, and re-layouts, per_device(): gathered = lax.all_gather(normed, 'tp', axis=0, tiled=True)  11.9 us
  transfers between devices with their start and end apart: 4, of which 4 were waited for; matrix products, arithmetic and copies ran while one was open for 16% of the time, Pallas kernels for 0%

profile of v1, /device:TPU:2, one launch (start us, length us, event | category | flops | bytes accessed | tf_op | source)
XLA Modules:
  0.0 543.0 jit_solution(5847224088328502347)
XLA Ops:
  6.5 0.0 all-gather.3.cloned.1.call-start
  6.5 1.2 fusion.10
  7.8 0.7 convert_element_type.34
  8.5 2.0 fusion.12
  10.5 0.0 all-gather.3.cloned.1.call-update
  10.6 0.0 all-gather.5.cloned.1.call-start
  10.6 1.0 constant_dynamic-slice_fusion.1
  11.6 2.0 pad_maximum_fusion
  13.6 0.0 all-gather.5.cloned.1.call-update
  13.7 5.2 stack.2
  18.9 0.0 copy-start.1
  18.9 11.6 %all-to-all-start = ((bf16[16,512,512]{2,1,0:T(8,128)(2,1)}), bf16[16,512,512]{2,1,0:T(8,128)(2,1)}, u32[]{:S(2)}, u32[]{:S(2)}) async-start(bf16[16,512,512]{2,1,0:T(8,128)(2,1)} %stack.2), calls=%async_computation | async-start | bytes 16777216 | tf_op jit(solution)/shard_map/all_to_all | solution.py:83
  30.5 0.0 reduce-scatter.2.cloned.1.call-start
  30.5 0.0 copy-done.1
  30.5 0.6 scatter_custom_fusion
  31.2 0.1 iota_compare_fusion
  31.3 0.5 fusion.22
  31.9 149.6 %all-gather.3.cloned.1.call-done = bf16[512,8192]{1,0:T(8,128)(2,1)} async-done(((bf16[32,8192]{1,0:T(8,128)(2,1)}), bf16[512,8192]{1,0:T(8,128)(2,1)}) %all-gather.3.cloned.1.call-update) | async-done | bytes 8388624 | tf_op jit(solution)/shard_map/all_gather | solution.py:58
  181.5 11.9 %copy.24 = bf16[512,8192]{0,1:T(8,128)(2,1)} copy(bf16[512,8192]{1,0:T(8,128)(2,1)} %all-gather.3.cloned.1.call-done) | data formatting | bytes 16777216 | tf_op jit(solution)/shard_map/all_gather | solution.py:58
  193.4 12.3 %copy.25 = bf16[512,16,512]{2,0,1:T(8,128)(2,1)} copy(bf16[512,16,512]{0,2,1:T(8,128)(2,1)} %bitcast.58) | data formatting | bytes 16777216 | tf_op jit(solution)/shard_map/reshape | solution.py:76
  205.7 8.2 %gather_fusion = bf16[16,512,512]{2,1,0:T(8,128)(2,1)} fusion(bf16[512,16,512]{2,0,1:T(8,128)(2,1)} %copy.25, s32[1024]{0:T(1024)S(1)} %pad_clamp_fusion.1), kind=kCustom, calls=%fused_computation.clone | custom fusion | bytes 16777280 | tf_op jit(solution)/shard_map/jit(_take)/gather | solution.py:79
  213.9 7.5 %select_bitcast_fusion.1 = bf16[512,16,512]{2,0,1:T(8,128)(2,1)} fusion(bf16[16,512,512]{2,1,0:T(8,128)(2,1)} %gather_fusion, pred[16]{0:T(512)(128)(4,1)S(1)} %compare_and_fusion.1), kind=kLoop, calls=%fused_computation.6 | loop fusion | flops 4194304 | bytes 16777232 | tf_op jit(solution)/shard_map/jit(_take)/select_n | solution.py:79
  221.3 12.3 %copy.26 = bf16[512,16,512]{0,2,1:T(8,128)(2,1)} copy(bf16[512,16,512]{2,0,1:T(8,128)(2,1)} %select_bitcast_fusion.1) | data formatting | bytes 16777216 | tf_op jit(solution)/shard_map/jit(_take)/select_n | solution.py:79
  233.6 34.9 %all-to-all-done = bf16[16,512,512]{2,1,0:T(8,128)(2,1)} async-done(((bf16[16,512,512]{2,1,0:T(8,128)(2,1)}), bf16[16,512,512]{2,1,0:T(8,128)(2,1)}, u32[]{:S(2)}, u32[]{:S(2)}) %all-to-all-start) | async-done | bytes 8388640 | tf_op jit(solution)/shard_map/all_to_all | solution.py:83
  268.5 8.3 %gather_fusion.1 = bf16[16,512,512]{2,1,0:T(8,128)(2,1)} fusion(bf16[512,16,512]{2,0,1:T(8,128)(2,1)} %bitcast.17, s32[1024]{0:T(1024)S(1)} %pad_clamp_fusion), kind=kCustom, calls=%fused_computation.1.clone | custom fusion | bytes 16777280 | tf_op jit(solution)/shard_map/jit(_take)/gather | solution.py:85
  276.8 7.6 %select_bitcast_fusion = bf16[512,16,512]{2,0,1:T(8,128)(2,1)} fusion(bf16[16,512,512]{2,1,0:T(8,128)(2,1)} %gather_fusion.1, pred[16]{0:T(512)(128)(4,1)S(1)} %compare_and_fusion), kind=kLoop, calls=%fused_computation.5 | loop fusion | flops 4194304 | bytes 16777232 | tf_op jit(solution)/shard_map/jit(_take)/select_n | solution.py:85
  284.4 11.8 %copy.32 = bf16[512,16,512]{0,2,1:T(8,128)(2,1)} copy(bf16[512,16,512]{2,0,1:T(8,128)(2,1)} %select_bitcast_fusion) | data formatting | bytes 16777216 | tf_op jit(solution)/shard_map/jit(_take)/select_n | solution.py:85
  296.1 78.7 %all-gather.5.cloned.1.call-done = bf16[8192,768]{1,0:T(8,128)(2,1)} async-done(((bf16[512,768]{1,0:T(8,128)(2,1)}), bf16[8192,768]{1,0:T(8,128)(2,1)}) %all-gather.5.cloned.1.call-update) | async-done | bytes 12582928 | tf_op jit(solution)/shard_map/all_gather | solution.py:14
  374.8 7.2 %slice_bitcast_fusion = bf16[512,8192]{0,1:T(8,128)(2,1)} fusion(bf16[8192,768]{1,0:T(8,128)(2,1)} %all-gather.5.cloned.1.call-done), kind=kLoop, calls=%fused_computation.4 | loop fusion | bytes 16777216 | tf_op jit(solution)/shard_map/dot_general | solution.py:80
  382.1 11.3 %copy.27 = bf16[512,8192]{1,0:T(8,128)(2,1)} copy(bf16[512,8192]{0,1:T(8,128)(2,1)} %slice_bitcast_fusion) | data formatting | bytes 16777216 | tf_op jit(solution)/shard_map/dot_general | solution.py:80
  393.4 0.0 copy-start
  393.4 7.1 %fusion = f32[512,256]{0,1:T(8,128)S(1)} fusion(bf16[512,8192]{0,1:T(8,128)(2,1)} %bitcast.60, bf16[8192,768]{1,0:T(8,128)(2,1)} %all-gather.5.cloned.1.call-done), kind=kOutput, calls=%fused_computation.7 | convolution fusion | flops 2147483648 | bytes 13107200 | tf_op jit(solution)/shard_map/dot_general | solution.py:81
  400.5 0.6 fusion.25
  401.1 0.0 copy-done
  401.1 7.3 %fusion.32 = f32[512,4,128]{0,2,1:T(8,128)S(1)} fusion(bf16[512,8192,1]{0,1,2:T(8,128)(2,1)} %bitcast.61, bf16[4,128,8192]{2,1,0:T(8,128)(2,1)S(1)} %bitcast.62), kind=kOutput, calls=%fused_computation.62 | convolution fusion | flops 4294967296 | bytes 17825792 | tf_op jit(solution)/shard_map/dot_general | solution.py:80
  408.4 0.2 subtract_convert_fusion
  408.6 0.9 fusion.3
  409.5 0.9 fusion.2
  410.4 1.5 fusion.7
  411.9 10.2 %convolution_convert_fusion = bf16[512,8192]{1,0:T(8,128)(2,1)} fusion(bf16[512,512]{0,1:T(8,128)(2,1)S(1)} %bitcast.63, bf16[512,8192]{0,1:T(8,128)(2,1)} %bitcast.59), kind=kOutput, calls=%fused_computation.3 | convolution fusion | flops 4299161600 | bytes 17301504 | tf_op jit(solution)/shard_map/dot_general | solution.py:95
  422.1 0.0 reduce-scatter.2.cloned.1.call-update
  422.1 114.3 %reduce-scatter.2.cloned.1.call-done = bf16[32,8192]{1,0:T(8,128)(2,1)} async-done(((bf16[512,8192]{1,0:T(8,128)(2,1)}), bf16[32,8192]{1,0:T(8,128)(2,1)}) %reduce-scatter.2.cloned.1.call-update) | async-done | bytes 524304 | tf_op jit(solution)/shard_map/reduce_scatter | solution.py:96
  (10 shorter events, 0.1 us)
Async XLA Ops:
  6.5 175.0 %all-gather.3.cloned.1.call-start = ((), (), s32[]{:S(2)}) async-start(), calls=%async_computation.2 | async-start | bytes 8912896 | tf_op jit(solution)/shard_map/all_gather | solution.py:58
  10.6 364.2 %all-gather.5.cloned.1.call-start = ((), (), s32[]{:S(2)}) async-start(), calls=%async_computation.3 | async-start | bytes 13369344 | tf_op jit(solution)/shard_map/all_gather | solution.py:14
  18.9 11.7 %copy-start.1 = (s32[16]{0:T(128)S(1)}, s32[16]{0:T(128)}, u32[]{:S(2)}) copy-start(s32[16]{0:T(128)} %param.13) | copy-start | bytes 196
  18.9 249.6 %all-to-all-start = ((bf16[16,512,512]{2,1,0:T(8,128)(2,1)}), bf16[16,512,512]{2,1,0:T(8,128)(2,1)}, u32[]{:S(2)}, u32[]{:S(2)}) async-start(bf16[16,512,512]{2,1,0:T(8,128)(2,1)} %stack.2), calls=%async_computation | async-start | bytes 16777216 | tf_op jit(solution)/shard_map/all_to_all | solution.py:83
  30.5 506.0 %reduce-scatter.2.cloned.1.call-start = ((), (), s32[]{:S(2)}) async-start(), calls=%async_computation.4 | async-start | bytes 8912896 | tf_op jit(solution)/shard_map/reduce_scatter | solution.py:96
  393.4 7.7 %copy-start = (bf16[512,8192]{1,0:T(8,128)(2,1)S(1)}, bf16[512,8192]{1,0:T(8,128)(2,1)}, u32[]{:S(2)}) copy-start(bf16[512,8192]{1,0:T(8,128)(2,1)} %copy.27) | copy-start | bytes 25165828
Sparse Core Ops, SparseCore 0:
  10.7 170.7 all-gather.2
  184.0 190.7 all-gather.4
  422.3 114.1 reduce-scatter.1
